TPU v7x, 256 devices: a whole 4x4x8 slice. The times are simulated.
256 devices in a mesh: row: 16 (over z_lo, y), col: 16 (over z_hi, x, core).
Axes of the slice: x: 4, y: 4, z: 8 (z_hi: 2, z_lo: 4; z = z_hi * 4 + z_lo), core: 2. Of those that a mesh axis runs over, the one named last changes fastest.
Arguments:
- features: bfloat16 [16384, 512], P(('row', 'col')), may hold values from -6 to 6
- w_first: bfloat16 [512, 512], replicated, may hold values from -0.25 to 0.25
- w_second: bfloat16 [512, 512], replicated, may hold values from -0.25 to 0.25
- block_index: int32 [16, 16, 64], P('row', 'col'), may hold values from 0 to 63, as said below
- block_count: int32 [16, 16], P('row', 'col'), may hold values from 0 to 16, as said below
- block_values: bfloat16 [16, 16, 64, 128, 128], P('row', 'col'), may hold values from -0.15625 to 0.15625
- cotangent: bfloat16 [16384, 512], P(('row', 'col')), may hold values from -0.046875 to 0.046875
Outputs:
- out_second: bfloat16 [16384, 512], P(('row', 'col'))
- grad_first: float32 [512, 512], replicated
- grad_second: float32 [512, 512], replicated
Inputs may be any that keep to these rules, and one draw needn't show every extreme that they name: `block_index`: in each tile the 64 slots name every block position p = r * 8 + c (block row r, block column c of the tile) once, in some order; the first block_count slots are the tile's nonzero blocks and the others are unused. `block_count`: nonzero blocks of each tile; in every draw some tile has exactly 16.
All inputs are finite; a program needn't handle non-finite values.
Results may differ from a plain program's by a relative error of at most 0.0061.
Values may be sent and summed in bfloat16 or wider, within the bound.
A program may use at most 64 MiB of HBM per device.

v0:
```python
import math

import jax
import jax.numpy as jnp
from jax import lax
from jax.sharding import PartitionSpec as P


def activate(v):
    return jax.nn.gelu(v, approximate=True)


def combine(tile_values, slot_index, slot_count, full_panel, flip):
    slots = slot_index.shape[0]
    block_size = tile_values.shape[-1]
    feat_width = full_panel.shape[1]
    in_blocks = full_panel.shape[0] // block_size
    if flip:
        col_blocks = slots // in_blocks
        out_blocks = col_blocks
    else:
        col_blocks = in_blocks
        out_blocks = slots // in_blocks
    group_size = math.gcd(slots, 32)
    panel_blocks = full_panel.reshape(in_blocks, block_size, feat_width)
    targets = jnp.arange(out_blocks, dtype=jnp.int32)
    offsets = jnp.arange(group_size, dtype=jnp.int32)

    def add_group(group_no, total):
        first_slot = group_no * group_size
        slot_ids = lax.dynamic_slice_in_dim(slot_index, first_slot, group_size, 0)
        group_values = lax.dynamic_slice_in_dim(tile_values, first_slot, group_size, 0)
        block_row = slot_ids // col_blocks
        block_col = slot_ids % col_blocks
        if flip:
            picked = panel_blocks[block_row]
            product = jnp.einsum(
                "sab,saf->sbf", group_values, picked, preferred_element_type=jnp.float32
            )
            target = block_col
        else:
            picked = panel_blocks[block_col]
            product = jnp.einsum(
                "sab,sbf->saf", group_values, picked, preferred_element_type=jnp.float32
            )
            target = block_row
        is_live = first_slot + offsets < slot_count
        onehot = ((target[None, :] == targets[:, None]) & is_live[None, :]).astype(jnp.float32)
        return total + jnp.einsum("os,saf->oaf", onehot, product, precision=lax.Precision.HIGHEST)

    groups = (slot_count + group_size - 1) // group_size
    total = lax.fori_loop(
        0, groups, add_group, jnp.zeros((out_blocks, block_size, feat_width), jnp.float32)
    )
    return total.reshape(out_blocks * block_size, feat_width)


def spread_rows(layer_input, tile_values, slot_index, slot_count):
    full_panel = lax.all_gather(layer_input, "row", axis=0, tiled=True)
    partial_value = combine(tile_values, slot_index, slot_count, full_panel, False)
    return lax.psum_scatter(partial_value, "col", scatter_dimension=0, tiled=True)


def spread_cols(layer_input, tile_values, slot_index, slot_count):
    full_panel = lax.all_gather(layer_input, "col", axis=0, tiled=True)
    partial_value = combine(tile_values, slot_index, slot_count, full_panel, True)
    return lax.psum_scatter(partial_value, "row", scatter_dimension=0, tiled=True)


def local(features, w_first, w_second, block_index, block_count, block_values, cotangent):
    slot_index = block_index[0, 0]
    slot_count = block_count[0, 0]
    tile_values = block_values[0, 0]
    first_linear = jnp.dot(features, w_first, preferred_element_type=jnp.float32).astype(
        jnp.bfloat16
    )
    first_sum = spread_cols(first_linear, tile_values, slot_index, slot_count)
    first_value, act_back = jax.vjp(activate, first_sum)
    first_active = first_value.astype(jnp.bfloat16)
    second_linear = jnp.dot(first_active, w_second, preferred_element_type=jnp.float32).astype(
        jnp.bfloat16
    )
    out_second = spread_rows(second_linear, tile_values, slot_index, slot_count).astype(
        jnp.bfloat16
    )
    back_second = spread_cols(cotangent, tile_values, slot_index, slot_count).astype(jnp.bfloat16)
    second_terms = jnp.einsum(
        "nf,ng->fg", first_active, back_second, preferred_element_type=jnp.float32
    )
    back_act = jnp.einsum("ng,fg->nf", back_second, w_second, preferred_element_type=jnp.float32)
    back_first = act_back(back_act)[0].astype(jnp.bfloat16)
    back_linear = spread_rows(back_first, tile_values, slot_index, slot_count).astype(jnp.bfloat16)
    first_terms = jnp.einsum("nf,ng->fg", features, back_linear, preferred_element_type=jnp.float32)
    grad_first, grad_second = lax.psum((first_terms, second_terms), ("row", "col"))
    return (out_second, grad_first, grad_second)


def solution(mesh):
    return jax.shard_map(
        local,
        mesh=mesh,
        in_specs=(
            P(("row", "col"), None),
            P(),
            P(),
            P("row", "col", None),
            P("row", "col"),
            P("row", "col", None, None, None),
            P(("row", "col"), None),
        ),
        out_specs=(P(("row", "col"), None), P(), P()),
        check_vma=False,
    )
```

profile of v0, /device:TPU:1, one launch (start us, length us, event | category | flops | bytes accessed | tf_op | source)
XLA Modules:
  0.0 913.9 jit_solution(1774365751613363130)
XLA Ops:
  10.7 60.3 %all-gather.5.cloned.1.call-done = bf16[1024,512]{1,0:T(8,128)(2,1)} async-done(((bf16[64,512]{1,0:T(8,128)(2,1)}), bf16[1024,512]{1,0:T(8,128)(2,1)}) %all-gather.5.cloned.1.call-update) | async-done | bytes 1048592 | tf_op jit(solution)/shard_map/all_gather | solution.py:65
  72.7 18.2 %while.52 = (s32[]{:T(128)}, f32[8,128,512]{2,0,1:T(8,128)}, s32[]{:T(128)}, s32[64]{0:T(128)}, s32[]{:T(128)}, /*index=5*/bf16[64,128,128]{2,1,0:T(8,128)(2,1)}...) while((s32[]{:T(128)}, f32[8,128,512]{2,0,1:T(8,128)}, ...), condition=%wide.region_1.2_spmd.clone, body=%wide.region_0.1_spmd.clone.sunk | while | flops 738724224 | bytes 42997128 | solution.py:52
  74.2 4.1 gather_fusion
  82.5 8.4 fusion.129
  90.9 4.3 copy.13
  95.3 29.7 %all-gather.9.cloned.1.call-done = bf16[1024,512]{1,0:T(8,128)(2,1)} async-done(((bf16[64,512]{1,0:T(8,128)(2,1)}), bf16[1024,512]{1,0:T(8,128)(2,1)}) %all-gather.9.cloned.1.call-update) | async-done | bytes 1048592 | tf_op jit(solution)/shard_map/all_gather | solution.py:65
  126.6 16.7 %while.54 = (s32[]{:T(128)}, f32[8,128,512]{2,0,1:T(8,128)}, s32[]{:T(128)}, s32[64]{0:T(128)S(1)}, s32[]{:T(128)}, /*index=5*/bf16[64,128,128]{2,1,0:T(8,128)(2...) while((s32[]{:T(128)}, f32[8,128,512]{2,0,1:T(8,128)}, ...), condition=%wide.region_7.8_spmd.clone, body=%wide.region_6.7_spmd.clone.sunk | while | flops 738724224 | bytes 34608496 | solution.py:52
  134.9 8.4 fusion.143
  143.3 4.2 copy.15
  147.6 53.5 %reduce-scatter.5.cloned.1.call-done = f32[64,512]{1,0:T(8,128)} async-done(((f32[1024,512]{1,0:T(8,128)}), f32[64,512]{1,0:T(8,128)}) %reduce-scatter.5.cloned.1.call-update) | async-done | bytes 131088 | tf_op jit(solution)/shard_map/reduce_scatter | solution.py:67
  201.1 87.2 %reduce-scatter.9.cloned.1.call-done = f32[64,512]{1,0:T(8,128)} async-done(((f32[1024,512]{1,0:T(8,128)}), f32[64,512]{1,0:T(8,128)}) %reduce-scatter.9.cloned.1.call-update) | async-done | bytes 131088 | tf_op jit(solution)/shard_map/reduce_scatter | solution.py:67
  292.2 75.2 %all-gather.11.cloned.1.call-done = bf16[1024,512]{1,0:T(8,128)(2,1)} async-done(((bf16[64,512]{1,0:T(8,128)(2,1)}), bf16[1024,512]{1,0:T(8,128)(2,1)}) %all-gather.11.cloned.1.call-update) | async-done | bytes 1048592 | tf_op jit(solution)/shard_map/all_gather | solution.py:59
  369.0 16.6 %while.55 = (s32[]{:T(128)}, f32[8,128,512]{2,0,1:T(8,128)}, s32[]{:T(128)}, s32[64]{0:T(128)S(1)}, s32[]{:T(128)}, /*index=5*/bf16[64,128,128]{2,1,0:T(8,128)(2...) while((s32[]{:T(128)}, f32[8,128,512]{2,0,1:T(8,128)}, ...), condition=%wide.region_10.11_spmd.clone, body=%wide.region_9.10_spmd.clone.sunk | while | flops 738724160 | bytes 34608360 | solution.py:52
  369.1 4.0 gather_fusion.3
  377.2 8.4 fusion.150
  385.6 4.2 copy.16
  389.9 58.9 %all-gather.7.cloned.1.call-done = bf16[1024,512]{1,0:T(8,128)(2,1)} async-done(((bf16[64,512]{1,0:T(8,128)(2,1)}), bf16[1024,512]{1,0:T(8,128)(2,1)}) %all-gather.7.cloned.1.call-update) | async-done | bytes 1048592 | tf_op jit(solution)/shard_map/all_gather | solution.py:59
  450.4 16.6 %while.53 = (s32[]{:T(128)}, f32[8,128,512]{2,0,1:T(8,128)}, s32[]{:T(128)}, s32[64]{0:T(128)S(1)}, s32[]{:T(128)}, /*index=5*/bf16[64,128,128]{2,1,0:T(8,128)(2...) while((s32[]{:T(128)}, f32[8,128,512]{2,0,1:T(8,128)}, ...), condition=%wide.region_4.5_spmd.clone, body=%wide.region_3.4_spmd.clone.sunk | while | flops 738724160 | bytes 34608360 | solution.py:52
  450.5 4.0 gather_fusion.1
  458.6 8.4 fusion.136
  467.0 4.2 copy.14
  472.7 74.9 %reduce-scatter.11.cloned.1.call-done = f32[64,512]{1,0:T(8,128)} async-done(((f32[1024,512]{1,0:T(8,128)}), f32[64,512]{1,0:T(8,128)}) %reduce-scatter.11.cloned.1.call-update) | async-done | bytes 131088 | tf_op jit(solution)/shard_map/reduce_scatter | solution.py:61
  549.8 85.9 %reduce-scatter.7.cloned.1.call-done = f32[64,512]{1,0:T(8,128)} async-done(((f32[1024,512]{1,0:T(8,128)}), f32[64,512]{1,0:T(8,128)}) %reduce-scatter.7.cloned.1.call-update) | async-done | bytes 131088 | tf_op jit(solution)/shard_map/reduce_scatter | solution.py:61
  637.2 265.4 %all-reduce.3.cloned.1.call-done = (f32[512,512]{0,1:T(8,128)}, f32[512,512]{1,0:T(8,128)}) async-done(((f32[512,512]{0,1:T(8,128)}, f32[512,512]{1,0:T(8,128)}), (f32[512,512]{0,1:T(8,128)}, f32[512,512]{1,0:T(8,128)})) %all-reduce.3.cloned.1.call-update) | async-done | bytes 2097168 | tf_op jit(solution)/shard_map/psum | solution.py:94
  (67 shorter events, 45.6 us)
Async XLA Ops:
  7.2 281.2 %copy-start = (bf16[512,512]{1,0:T(8,128)(2,1)S(1)}, bf16[512,512]{1,0:T(8,128)(2,1)}, u32[]{:S(2)}) copy-start(bf16[512,512]{1,0:T(8,128)(2,1)} %param.17) | copy-start | bytes 1572868
  7.2 63.8 %all-gather.5.cloned.1.call-start = ((), (), s32[]{:S(2)}) async-start(), calls=%async_computation.4 | async-start | bytes 1114112 | tf_op jit(solution)/shard_map/all_gather | solution.py:65
  9.2 115.7 %all-gather.9.cloned.1.call-start = ((), (), s32[]{:S(2)}) async-start(), calls=%async_computation.8 | async-start | bytes 1114112 | tf_op jit(solution)/shard_map/all_gather | solution.py:65
  10.0 191.2 %reduce-scatter.5.cloned.1.call-start = ((), (), s32[]{:S(2)}) async-start(), calls=%async_computation.5 | async-start | bytes 2228224 | tf_op jit(solution)/shard_map/reduce_scatter | solution.py:67
  74.2 4.2 copy-start.2
  90.9 35.7 %copy-start.3 = (bf16[64,128,128]{2,1,0:T(8,128)(2,1)S(1)}, bf16[64,128,128]{2,1,0:T(8,128)(2,1)}, u32[]{:S(2)}) copy-start(bf16[64,128,128]{2,1,0:T(8,128)(2,1)} %get-tuple-element.970) | copy-start | bytes 6291460
  90.9 35.7 %copy-start.5 = (s32[64]{0:T(128)S(1)}, s32[64]{0:T(128)}, u32[]{:S(2)}) copy-start(s32[64]{0:T(128)} %get-tuple-element.988) | copy-start | bytes 772
  95.2 193.2 %reduce-scatter.9.cloned.1.call-start = ((), (), s32[]{:S(2)}) async-start(), calls=%async_computation.9 | async-start | bytes 2228224 | tf_op jit(solution)/shard_map/reduce_scatter | solution.py:67
  147.6 219.8 %all-gather.11.cloned.1.call-start = ((), (), s32[]{:S(2)}) async-start(), calls=%async_computation.10 | async-start | bytes 1114112 | tf_op jit(solution)/shard_map/all_gather | solution.py:59
  290.3 158.4 %all-gather.7.cloned.1.call-start = ((), (), s32[]{:S(2)}) async-start(), calls=%async_computation.6 | async-start | bytes 1114112 | tf_op jit(solution)/shard_map/all_gather | solution.py:59
  292.1 255.4 %reduce-scatter.11.cloned.1.call-start = ((), (), s32[]{:S(2)}) async-start(), calls=%async_computation.11 | async-start | bytes 2228224 | tf_op jit(solution)/shard_map/reduce_scatter | solution.py:61
  389.8 245.8 %reduce-scatter.7.cloned.1.call-start = ((), (), s32[]{:S(2)}) async-start(), calls=%async_computation.7 | async-start | bytes 2228224 | tf_op jit(solution)/shard_map/reduce_scatter | solution.py:61
  467.0 4.3 copy-start.4
  467.0 4.3 copy-start.7
  467.0 80.5 %copy-start.6 = (bf16[64,512]{1,0:T(8,128)(2,1)S(1)}, bf16[64,512]{1,0:T(8,128)(2,1)}, u32[]{:S(2)}) copy-start(bf16[64,512]{1,0:T(8,128)(2,1)} %param.15) | copy-start | bytes 196612
  471.3 431.3 %all-reduce.3.cloned.1.call-start = ((), (), s32[]{:S(2)}) async-start(), calls=%async_computation.12 | async-start | bytes 4194304 | tf_op jit(solution)/shard_map/psum | solution.py:94
  471.3 436.0 %copy-start.1 = (bf16[512,512]{1,0:T(8,128)(2,1)S(1)}, bf16[512,512]{1,0:T(8,128)(2,1)}, u32[]{:S(2)}) copy-start(bf16[512,512]{1,0:T(8,128)(2,1)} %param.17) | copy-start | bytes 1572868
Sparse Core Ops, SparseCore 0:
  11.3 59.6 all-gather.4
  73.7 51.1 all-gather.8
  127.5 73.6 reduce-scatter.4
  203.5 84.8 reduce-scatter.8
  290.6 76.7 all-gather.10
  369.6 79.1 all-gather.6
  453.0 94.4 reduce-scatter.10
  551.8 83.8 reduce-scatter.6
  641.8 260.7 all-reduce.2
where the time goes:
time: 915 us; the launch traced here: 914 us
  waiting for transfers between devices  792 us (87%)
  matrix products  56.6 us (6%)
  local copies, waits for them, and re-layouts  44.5 us (5%)
  between operations  14.6 us (2%)
    psum x1, waiting for transfers between devices, local(): lax.psum((first_terms, second_terms), ('row', 'col'))  265 us
    reduce_scatter x2, waiting for transfers between devices, spread_rows(): lax.psum_scatter(partial_value, 'col', scatter_dimension=0, tiled=True)  161 us
    reduce_scatter x2, waiting for transfers between devices, spread_cols(): lax.psum_scatter(partial_value, 'row', scatter_dimension=0, tiled=True)  141 us
    all_gather x2, waiting for transfers between devices, spread_rows(): full_panel = lax.all_gather(layer_input, 'row', axis=0, tiled=True)  134 us
    all_gather x2, waiting for transfers between devices, spread_cols(): full_panel = lax.all_gather(layer_input, 'col', axis=0, tiled=True)  90 us
    dot_general x4, matrix products, add_group(): jnp.einsum('os,saf->oaf', onehot, product, precision=lax.Precision.HIGHEST)  33.7 us
  transfers between devices with their start and end apart: 9, of which 9 were waited for; matrix products, arithmetic and copies ran while one was open for 11% of the time, Pallas kernels for 0%

commit v1 on v0

v1 whole, which is shorter than its diff:
```python
import jax
import jax.numpy as jnp
from jax import lax
from jax.experimental import pallas as pl
from jax.experimental.pallas import tpu as pltpu
from jax.sharding import PartitionSpec as P

MESH = pl.DeviceIdType.MESH
BF = jnp.bfloat16
F32 = jnp.float32
ROWS = 64
WIDTH = 512
LIVE = 16
GELU_A = 0.7978845608
GELU_B = 0.044715


def dot(a, b):
    return jnp.dot(a, b, preferred_element_type=F32)


def kernel(
    table, feat, cot, w1_hbm, w2_hbm, vals_hbm, out_hbm, grad_hbm,
    X, PT, RY, Q, RZ, Y, PO, RK, Q2, RX, Q3, RH, S, ST, V, VT, W1, W2,
    GS, GB, TG, GT, RGX, GY, RGY, GZ, RGZ, FZ, FG, ACT, OUT, KEEP,
    ssem, rsX, rsRY, rsRZ, rsY, rsRK, rsRX, rsRH, rsGB, rsRGX, rsRGY, rsRGZ, rsFZ, rsFY, rsFX, rsFK, lsem,
):
    r = lax.axis_index("row")
    c = lax.axis_index("col")
    z, y = r // 4, r % 4
    h, x, k = c // 8, (c // 2) % 4, c % 2
    q = h * 4 + z
    nh, nk = 1 - h, 1 - k

    def dev(z=z, y=y, h=h, x=x, k=k):
        return (z * 4 + y, h * 8 + x * 2 + k)

    xs = [(x + d) % 4 for d in (1, 3, 2)]
    ys = [(y + d) % 4 for d in (1, 3, 2)]
    zs = [(z + d) % 4 for d in (1, 2, 3)]
    qs = [(q + d) % 8 for d in (4, 3, 5, 2, 6, 1, 7)]
    core = dev(k=nk)
    dx = [dev(x=v) for v in xs]
    dy = [dev(y=v) for v in ys]
    dz = [dev(z=v) for v in zs]
    dq = [dev(z=v % 4, h=v // 4) for v in qs]
    anti = dev(h=nh)

    sends = []

    def send(src, dst, rsem, target):
        n = len(sends)
        cp = pltpu.make_async_remote_copy(
            src_ref=src, dst_ref=dst, send_sem=ssem.at[n], recv_sem=rsem, device_id=target, device_id_type=MESH
        )
        cp.start()
        sends.append(cp)

    def got(dst, rsem):
        pltpu.make_async_remote_copy(
            src_ref=dst, dst_ref=dst, send_sem=ssem.at[0], recv_sem=rsem, device_id=core, device_id_type=MESH
        ).wait_recv()

    loads = [
        pltpu.make_async_copy(feat, X.at[0, c], lsem.at[0]),
        pltpu.make_async_copy(cot, X.at[1, c], lsem.at[1]),
        pltpu.make_async_copy(vals_hbm.at[pl.ds(0, LIVE)], V.at[pl.ds(0, LIVE)], lsem.at[2]),
        pltpu.make_async_copy(w1_hbm, W1, lsem.at[3]),
        pltpu.make_async_copy(w2_hbm, W2, lsem.at[4]),
    ]
    for cp in loads:
        cp.start()

    barrier = pltpu.get_barrier_semaphore()
    partners = [core] + dx + dy + dq
    for target in partners:
        pl.semaphore_signal(barrier, inc=1, device_id=target, device_id_type=MESH)
    pl.semaphore_wait(barrier, len(partners))

    def slot(h, x, k):
        return h * 8 + x * 2 + k

    def spread(a, s, targets):
        for t in targets:
            send(X.at[a, s], X.at[a, s], rsX.at[a * 16 + s], t)

    def have(a, s):
        got(X.at[a, s], rsX.at[a * 16 + s])

    for a in range(2):
        loads[a].wait()
        spread(a, c, [anti] + dx + [core])

    loads[2].wait()
    V[LIVE] = jnp.zeros((128, 128), BF)
    VT[LIVE] = jnp.zeros((128, 128), BF)

    def flip(s, carry):
        VT[s] = V[s].T
        return carry

    lax.fori_loop(0, LIVE, flip, 0)

    def place(i, carry):
        for j in range(8):
            S[i, :, j * 128 : (j + 1) * 128] = V[table[i * 8 + j]]
            ST[i, :, j * 128 : (j + 1) * 128] = VT[table[j * 8 + i]]
        return carry

    lax.fori_loop(0, 8, place, 0)

    for a in range(2):
        s = slot(nh, x, k)
        have(a, s)
        spread(a, s, dx + [core])

    for a in range(2):
        for hh in (h, nh):
            for v in xs:
                s = slot(hh, v, k)
                have(a, s)
                spread(a, s, [core])
        for hh in (h, nh):
            for v in [x] + xs:
                have(a, slot(hh, v, nk))
        for j in zs + [z]:
            lhs = ST[pl.ds(2 * j, 2)].reshape(256, 1024)
            prod = dot(lhs, X[a].reshape(1024, WIDTH))
            PT[a, j] = prod.astype(BF).reshape(4, ROWS, WIDTH)
            for v, t in zip(ys, dy):
                send(PT.at[a, j, v], RY.at[a, y, j], rsRY.at[a * 16 + y * 4 + j], t)

    def reduce_y(a):
        for j, t in zip(zs + [z], dz + [None]):
            total = PT[a, j, y].astype(F32)
            for v in ys:
                got(RY.at[a, v, j], rsRY.at[a * 16 + v * 4 + j])
                total += RY[a, v, j].astype(F32)
            if t is None:
                KEEP[...] = total
            else:
                Q[a, j] = total.astype(BF)
                send(Q.at[a, j], RZ.at[a, z], rsRZ.at[a * 4 + z], t)

    def reduce_z(a):
        total = KEEP[...]
        for v in zs:
            got(RZ.at[a, v], rsRZ.at[a * 4 + v])
            total += RZ[a, v].astype(F32)
        return total

    reduce_y(0)
    agg = reduce_z(0)
    loads[3].wait()
    loads[4].wait()
    agg_hi = agg.astype(BF)
    agg_lo = (agg - agg_hi.astype(F32)).astype(BF)
    both = dot(jnp.concatenate([agg_hi, agg_lo], axis=0), W1[...])
    v1 = both[:ROWS] + both[ROWS:]
    th = jnp.tanh(GELU_A * (v1 + GELU_B * v1 * v1 * v1))
    act = (0.5 * v1 * (1.0 + th)).astype(BF)
    dact = 0.5 * (1.0 + th) + 0.5 * v1 * (1.0 - th * th) * GELU_A * (1.0 + 3.0 * GELU_B * v1 * v1)
    Y[r] = dot(act, W2[...]).astype(BF)
    for t in dz + dy:
        send(Y.at[r], Y.at[r], rsY.at[r], t)
    ACT[0] = dact
    GB[0, 0] = jnp.where(k == 0, agg_hi, act)
    GB[0, 1] = jnp.where(k == 0, agg_lo, jnp.zeros_like(agg_lo))
    GS[0] = jnp.where(k == 0, act, agg_hi)
    GS[1] = jnp.where(k == 0, jnp.zeros_like(agg_lo), agg_lo)

    reduce_y(1)
    for v in zs:
        s = v * 4 + y
        got(Y.at[s], rsY.at[s])
        for t in dy:
            send(Y.at[s], Y.at[s], rsY.at[s], t)
    bs = reduce_z(1).astype(BF)
    back = lax.dot_general(bs, W2[...], (((1,), (1,)), ((), ())), preferred_element_type=F32)
    bf = (back * ACT[0]).astype(BF)
    GB[0, 2] = jnp.where(k == 0, bf, bs)
    GS[2] = jnp.where(k == 0, bs, bf)
    send(GS, GB.at[1], rsGB.at[0], core)
    got(GB.at[1], rsGB.at[0])

    lhs = jnp.concatenate([GB[0, 0], GB[0, 1], GB[1, 0], GB[1, 1]], axis=0)
    rhs = jnp.concatenate([GB[0, 2], GB[0, 2], GB[1, 2], GB[1, 2]], axis=0)
    terms = lax.dot_general(lhs, rhs, (((0,), (0,)), ((), ())), preferred_element_type=F32)
    TG[...] = terms.reshape(4, 128, WIDTH)
    GT[...] = terms.astype(BF).reshape(4, 128, WIDTH)
    for v, t in zip(xs, dx):
        send(GT.at[v], RGX.at[x], rsRGX.at[x], t)

    for zz in zs + [z]:
        for v in ys:
            s = zz * 4 + v
            got(Y.at[s], rsY.at[s])
    for i in range(4):
        prod = dot(S[pl.ds(2 * i, 2)].reshape(256, 1024), Y[...].reshape(1024, WIDTH))
        PO[pl.ds(4 * i, 4)] = prod.astype(BF).reshape(4, ROWS, WIDTH)
        for g in range(2):
            b = 2 * i + g
            send(PO.at[2 * b + nk], RK.at[b], rsRK.at[b], core)

    for hh in (nh, h):
        for v, t in zip(xs + [x], dx + [None]):
            b = hh * 4 + v
            got(RK.at[b], rsRK.at[b])
            Q2[b] = (PO[2 * b + k].astype(F32) + RK[b].astype(F32)).astype(BF)
            if t is not None:
                send(Q2.at[b], RX.at[x, hh], rsRX.at[x * 2 + hh], t)

    total = TG[x]
    for v in xs:
        got(RGX.at[v], rsRGX.at[v])
        total += RGX[v].astype(F32)
    GY[...] = total.reshape(4, 32, WIDTH)
    for v, t in zip(ys, dy):
        send(GY.at[v], RGY.at[y], rsRGY.at[y], t)

    for hh in (nh, h):
        total = Q2[hh * 4 + x].astype(F32)
        for v in xs:
            got(RX.at[v, hh], rsRX.at[v * 2 + hh])
            total += RX[v, hh].astype(F32)
        if hh is nh:
            Q3[...] = total.astype(BF)
            send(Q3, RH, rsRH.at[0], anti)
        else:
            KEEP[...] = total

    total = GY[y]
    for v in ys:
        got(RGY.at[v], rsRGY.at[v])
        total += RGY[v]
    for i in range(4):
        for j in range(2):
            GZ[2 * i + j] = total[8 * i : 8 * i + 8, 256 * j : 256 * j + 256]
    for v, t in zip(qs, dq):
        send(GZ.at[v], RGZ.at[q], rsRGZ.at[q], t)

    got(RH, rsRH.at[0])
    OUT[...] = (KEEP[...] + RH[...].astype(F32)).astype(BF)
    store_out = pltpu.make_async_copy(OUT, out_hbm, lsem.at[5])
    store_out.start()

    total = GZ[q]
    for v in qs:
        got(RGZ.at[v], rsRGZ.at[v])
        total += RGZ[v]
    FZ[q] = total
    for t in dq:
        send(FZ.at[q], FZ.at[q], rsFZ.at[q], t)
    for v in qs:
        got(FZ.at[v], rsFZ.at[v])
    rows = []
    for i in range(4):
        rows.append(jnp.concatenate([FZ[2 * i], FZ[2 * i + 1]], axis=1))
    FG[k, x, y] = jnp.concatenate(rows, axis=0).astype(BF)
    for t in dy:
        send(FG.at[k, x, y], FG.at[k, x, y], rsFY.at[y], t)
    for v in ys:
        got(FG.at[k, x, v], rsFY.at[v])
    for t in dx + [core]:
        send(FG.at[k, x], FG.at[k, x], rsFX.at[k * 4 + x], t)
    for v in xs:
        got(FG.at[k, v], rsFX.at[k * 4 + v])
        send(FG.at[k, v], FG.at[k, v], rsFX.at[k * 4 + v], core)
    store_own = pltpu.make_async_copy(FG.at[k], grad_hbm.at[k], lsem.at[6])
    store_own.start()
    for v in [x] + xs:
        got(FG.at[nk, v], rsFX.at[nk * 4 + v])
    store_other = pltpu.make_async_copy(FG.at[nk], grad_hbm.at[nk], lsem.at[7])
    store_other.start()
    for cp in sends:
        cp.wait_send()
    store_out.wait()
    store_own.wait()
    store_other.wait()


def local(features, w_first, w_second, block_index, block_count, block_values, cotangent):
    index = block_index[0, 0][:LIVE]
    count = block_count[0, 0]
    ids = jnp.arange(LIVE, dtype=jnp.int32)
    places = jnp.arange(64, dtype=jnp.int32)
    hit = (index[None, :] == places[:, None]) & (ids < count)[None, :]
    table = LIVE + jnp.sum(jnp.where(hit, ids[None, :] - LIVE, 0), axis=1, dtype=jnp.int32)
    anyspace = pl.BlockSpec(memory_space=pl.ANY)
    vm = pltpu.VMEM
    dma = pltpu.SemaphoreType.DMA
    piece = (ROWS, WIDTH)
    out, grads = pl.pallas_call(
        kernel,
        name="gcn",
        out_shape=(
            jax.ShapeDtypeStruct(piece, BF),
            jax.ShapeDtypeStruct((2, 4, 4, 32, WIDTH), BF),
        ),
        in_specs=[pl.BlockSpec(memory_space=pltpu.SMEM)] + [anyspace] * 5,
        out_specs=(anyspace, anyspace),
        scratch_shapes=[
            vm((2, 16) + piece, BF),
            vm((2, 4, 4) + piece, BF),
            vm((2, 4, 4) + piece, BF),
            vm((2, 4) + piece, BF),
            vm((2, 4) + piece, BF),
            vm((16,) + piece, BF),
            vm((16,) + piece, BF),
            vm((8,) + piece, BF),
            vm((8,) + piece, BF),
            vm((4, 2) + piece, BF),
            vm(piece, BF),
            vm(piece, BF),
            vm((8, 128, 1024), BF),
            vm((8, 128, 1024), BF),
            vm((LIVE + 1, 128, 128), BF),
            vm((LIVE + 1, 128, 128), BF),
            vm((WIDTH, WIDTH), BF),
            vm((WIDTH, WIDTH), BF),
            vm((3,) + piece, BF),
            vm((2, 3) + piece, BF),
            vm((4, 128, WIDTH), F32),
            vm((4, 128, WIDTH), BF),
            vm((4, 128, WIDTH), BF),
            vm((4, 32, WIDTH), F32),
            vm((4, 32, WIDTH), F32),
            vm((8, 8, 256), F32),
            vm((8, 8, 256), F32),
            vm((8, 8, 256), F32),
            vm((2, 4, 4, 32, WIDTH), BF),
            vm((1,) + piece, F32),
            vm(piece, BF),
            vm(piece, F32),
            dma((160,)),
            dma((32,)), dma((32,)), dma((8,)), dma((16,)), dma((8,)), dma((8,)), dma((1,)), dma((1,)),
            dma((4,)), dma((4,)), dma((8,)), dma((8,)), dma((4,)), dma((8,)), dma((1,)), dma((8,)),
        ],
        compiler_params=pltpu.CompilerParams(collective_id=0, has_side_effects=True, vmem_limit_bytes=48 << 20),
    )(table, features, cotangent, w_first, w_second, block_values[0, 0])
    grads = grads.reshape(2, WIDTH, WIDTH).astype(F32)
    return out, grads[0], grads[1]


def solution(mesh):
    return jax.shard_map(
        local,
        mesh=mesh,
        in_specs=(
            P(("row", "col"), None),
            P(),
            P(),
            P("row", "col", None),
            P("row", "col"),
            P("row", "col", None, None, None),
            P(("row", "col"), None),
        ),
        out_specs=(P(("row", "col"), None), P(), P()),
        check_vma=False,
    )
```

time: 915 us -> 106 us (0.12)
  waiting for transfers between devices: 792 us -> 0 us
  Pallas kernels: 0 us -> 96.3 us
  matrix products: 56.6 us -> 0 us
  local copies, waits for them, and re-layouts: 44.5 us -> 8.23 us
  between operations: 14.6 us -> 1.31 us
    reduce_scatter x4 -> x0, waiting for transfers between devices: 302 us -> none  [the longest x2 161 us: spread_rows(): lax.psum_scatter(partial_value, 'col', scatter_dimension=0, tiled=True)]
    psum x1 -> x0, waiting for transfers between devices: 265 us -> none  [local(): lax.psum((first_terms, second_terms), ('row', 'col'))]
    all_gather x4 -> x0, waiting for transfers between devices: 224 us -> none  [the longest x2 134 us: spread_rows(): full_panel = lax.all_gather(layer_input, 'row', axis=0, tiled=True)]
    pallas_call x0 -> x1, Pallas kernels: none -> 96.3 us  [local(): pl.pallas_call(kernel, name='gcn', out_shape=(jax.ShapeDtypeStruct(piece,...]
    dot_general x13 -> x0, matrix products: 56.6 us -> none  [the longest x4 33.7 us: add_group(): jnp.einsum('os,saf->oaf', onehot, product, precision=lax.Precision.HIGHEST)]
    while x6 -> x0, local copies, waits for them, and re-layouts: 16.9 us -> none  [the longest x4 16.9 us: combine(): lax.fori_loop(0, groups, add_group, jnp.zeros((out_blocks, block_size, fe...]
    gather x4 -> x0, local copies, waits for them, and re-layouts: 16.1 us -> none  [the longest x2 8.13 us: add_group(): picked = panel_blocks[block_row]]
  transfers between devices with their start and end apart: 9 -> 0, of which waited for: 9 -> 0; matrix products, arithmetic and copies ran while one was open for 11% -> 0% of each run, Pallas kernels for 0% -> 0%
where the time goes in v1:
time: 106 us
  Pallas kernels  96.3 us (91%)
  local copies, waits for them, and re-layouts  8.23 us (8%)
  between operations  1.31 us (1%)
    pallas_call x1, Pallas kernels, local(): pl.pallas_call(kernel, name='gcn', out_shape=(jax.ShapeDtypeStruct(piece,...  96.3 us
    unnamed x11, local copies, waits for them, and re-layouts  5.97 us

profile of v1, /device:TPU:1, one launch (start us, length us, event | category | flops | bytes accessed | tf_op | source)
XLA Modules:
  0.0 105.9 jit_solution(2600749540767870028)
XLA Ops:
  1.3 0.7 slice_bitcast_fusion
  2.0 0.1 select_reduce_fusion
  2.0 0.0 copy-start
  2.1 1.6 %copy-done = bf16[1,1,64,128,128]{4,3,2,1,0:T(8,128)(2,1)S(1)} copy-done((bf16[1,1,64,128,128]{4,3,2,1,0:T(8,128)(2,1)S(1)}, bf16[1,1,64,128,128]{4,3,2,1,0:T(8,128)(2,1)}, u32[]{:S(2)}) %copy-start) | copy-done | bytes 2097176
  3.6 0.0 copy-start.1
  3.6 1.0 copy-done.1
  4.7 0.0 copy-start.2
  4.7 1.0 copy-done.2
  5.7 0.0 copy-start.3
  5.7 0.8 copy-done.3
  6.6 0.0 copy-start.4
  6.6 0.8 copy-done.4
  7.4 96.3 %gcn.1 = (bf16[64,512]{1,0:T(8,128)(2,1)S(1)}, bf16[2,4,4,32,512]{4,3,2,1,0:T(8,128)(2,1)S(1)}) custom-call(s32[64]{0:T(128)S(1)} %broadcast_add_fusion.table, bf16[64,512]{1,0:T(8,128)(2,1)S(1)} %copy-done.3, bf16[64,512]{1,0:T(8,128)(2,1)S(1)} %copy-done.4, bf16[512,512]{1,0:T(8,128)(2,1)S(1)} %copy-done.1, bf16[512,512]{1,0:T(8,128)(2,1)S(1)} %copy-done.2, ...), custom_call_target="tpu_custom_call" | custom-call | tf_op jit(solution)/shard_map/gcn/pallas_call | solution.py:293
  103.7 1.6 %fusion.1 = (f32[1,4,4,32,512]{4,3,2,1,0:T(8,128)}, f32[1,4,4,32,512]{4,3,2,1,0:T(8,128)}) fusion(bf16[2,4,4,32,512]{4,3,2,1,0:T(8,128)(2,1)S(1)} %get-tuple-element.6), kind=kLoop, calls=%fused_computation.7 | loop fusion | bytes 4194304 | tf_op jit(solution)/shard_map/slice | solution.py:342
  105.3 0.6 copy.12
  (3 shorter events, 0.0 us)
Async XLA Ops:
  2.0 1.6 %copy-start = (bf16[1,1,64,128,128]{4,3,2,1,0:T(8,128)(2,1)S(1)}, bf16[1,1,64,128,128]{4,3,2,1,0:T(8,128)(2,1)}, u32[]{:S(2)}) copy-start(bf16[1,1,64,128,128]{4,3,2,1,0:T(8,128)(2,1)} %param.12) | copy-start | bytes 6291460
  3.6 1.0 copy-start.1
  4.7 1.0 copy-start.2
  5.7 0.8 copy-start.3
  6.6 0.8 copy-start.4

commit v2 on v1

v2 whole, which is shorter than its diff:
```python
import jax
import jax.numpy as jnp
from jax import lax
from jax.experimental import pallas as pl
from jax.experimental.pallas import tpu as pltpu
from jax.sharding import PartitionSpec as P

MESH = pl.DeviceIdType.MESH
BF = jnp.bfloat16
F32 = jnp.float32
ROWS = 64
WIDTH = 512
LIVE = 16
GELU_A = 0.7978845608
GELU_B = 0.044715


def dot(a, b):
    return jnp.dot(a, b, preferred_element_type=F32)


NCH = 2
NSEND = 320
CW = 512
HALF = ROWS // 2


def kernel(
    table, feat, cot, w1_hbm, w2_hbm, vals_hbm, out_hbm, grad_hbm,
    X, PT, RA, RB, Q, RZ, KEEP, Y, PO, RK, Q2, OX, Q3, RH, S, ST, V, VT, W1, W2,
    GS, GB, GT, GR, GY, RGY, GZ, RGZ, FZ, FG, ACT, OUT,
    ssem, rsX, rsXH, rsA, rsB, rsRZ, rsY, rsRK, rsOX, rsRH, rsGB, rsGR, rsRGY, rsRGZ,
    rsFZ, rsFY, rsFX, rsFK, lsem,
):
    r = lax.axis_index("row")
    c = lax.axis_index("col")
    z, y = r // 4, r % 4
    h, x, k = c // 8, (c // 2) % 4, c % 2
    q = h * 4 + z
    nh, nk = 1 - h, 1 - k

    def dev(z=z, y=y, h=h, x=x, k=k):
        return (z * 4 + y, h * 8 + x * 2 + k)

    xp, xm, xa = (x + 1) % 4, (x + 3) % 4, (x + 2) % 4
    yp, ym, ya = (y + 1) % 4, (y + 3) % 4, (y + 2) % 4
    zs = [(z + d) % 4 for d in (1, 2, 3)]
    ys = [yp, ym, ya]
    qs = [(q + d) % 8 for d in (4, 3, 5, 2, 6, 1, 7)]
    core = dev(k=nk)
    dxp, dxm = dev(x=xp), dev(x=xm)
    xs = [xp, xm, xa]
    dx = [dxp, dxm, dev(x=xa)]
    dyp, dym = dev(y=yp), dev(y=ym)
    dy = [dyp, dym, dev(y=ya)]
    dz = [dev(z=v) for v in zs]
    dq = [dev(z=v % 4, h=v // 4) for v in qs]
    anti = dev(h=nh)

    sends = []

    def send(src, dst, rsem, target):
        n = len(sends)
        cp = pltpu.make_async_remote_copy(
            src_ref=src, dst_ref=dst, send_sem=ssem.at[n], recv_sem=rsem, device_id=target, device_id_type=MESH
        )
        cp.start()
        sends.append(cp)

    def got(dst, rsem):
        pltpu.make_async_remote_copy(
            src_ref=dst, dst_ref=dst, send_sem=ssem.at[0], recv_sem=rsem, device_id=core, device_id_type=MESH
        ).wait_recv()

    def ring_start(at, p, m, o, up, down, ra, rb, sa, sb, n):
        send(at(o).at[:n], ra.at[0], sa(0), up)
        send(at(o).at[n:], ra.at[1], sa(1), down)
        send(at(p).at[n:], rb.at[0, n:], sb(0), up)
        send(at(m).at[:n], rb.at[1, :n], sb(1), down)

    def ring_relay(at, p, m, up, down, ra, rb, sa, sb, n):
        got(ra.at[0], sa(0))
        at(p)[:n] = (at(p)[:n].astype(F32) + ra[0].astype(F32)).astype(BF)
        send(at(p).at[:n], rb.at[0, :n], sb(2), up)
        got(ra.at[1], sa(1))
        at(m)[n:] = (at(m)[n:].astype(F32) + ra[1].astype(F32)).astype(BF)
        send(at(m).at[n:], rb.at[1, n:], sb(3), down)

    def ring_sum(rb, sb, n):
        got(rb.at[0, n:], sb(0))
        got(rb.at[1, :n], sb(1))
        got(rb.at[0, :n], sb(2))
        got(rb.at[1, n:], sb(3))
        return rb[0].astype(F32) + rb[1].astype(F32)

    loads = []
    for a in range(NCH):
        for i in range(2):
            src = (feat, cot)[a].at[pl.ds(i * HALF, HALF)]
            loads.append(pltpu.make_async_copy(src, X.at[a, c, i], lsem.at[2 * a + i]))
    loads += [
        pltpu.make_async_copy(vals_hbm.at[pl.ds(0, LIVE)], V.at[pl.ds(0, LIVE)], lsem.at[10]),
        pltpu.make_async_copy(w1_hbm, W1, lsem.at[4]),
        pltpu.make_async_copy(w2_hbm, W2, lsem.at[5]),
    ]
    for cp in loads:
        cp.start()

    barrier = pltpu.get_barrier_semaphore()
    partners = [core] + dx + dy + dq
    for target in partners:
        pl.semaphore_signal(barrier, inc=1, device_id=target, device_id_type=MESH)
    pl.semaphore_wait(barrier, len(partners))

    def slot(h, x, k):
        return h * 8 + x * 2 + k

    def spread(a, s, targets, halves=(0, 1)):
        for i in halves if a == 0 else ():
            for t in targets:
                send(X.at[0, s, i], X.at[0, s, i], rsX.at[i * 16 + s], t)
        for t in targets if a == 1 else ():
            send(X.at[1, s], X.at[1, s], rsX.at[32 + s], t)

    def have(a, s, halves=(0, 1)):
        for i in halves if a == 0 else ():
            got(X.at[0, s, i], rsX.at[i * 16 + s])
        if a == 1:
            got(X.at[1, s], rsX.at[32 + s])

    for i in range(2):
        loads[i].wait()
        spread(0, c, [anti], (i,))
    spread(0, c, dx + [core])
    loads[2].wait()
    loads[3].wait()
    spread(1, c, [anti, core])

    loads[4].wait()
    V[LIVE] = jnp.zeros((128, 128), BF)
    VT[LIVE] = jnp.zeros((128, 128), BF)

    def flip(s, carry):
        VT[s] = V[s].T
        return carry

    lax.fori_loop(0, LIVE, flip, 0)

    def place(i, carry):
        for j in range(8):
            S[i, :, j * 128 : (j + 1) * 128] = V[table[i * 8 + j]]
            ST[i, :, j * 128 : (j + 1) * 128] = VT[table[j * 8 + i]]
        return carry

    lax.fori_loop(0, 8, place, 0)

    def across(a, halves=(0, 1)):
        s = slot(nh, x, k)
        for i in halves:
            have(a, s, (i,))
            spread(a, s, (dx if a == 0 else [dxp, dxm]) + [core], (i,))

    def half_sem(hh, i):
        return rsXH.at[hh * 2 + i]

    def near(hh):
        s = slot(hh, xm, k)
        have(1, s)
        send(X.at[1, s, 0], X.at[1, s, 0], half_sem(hh, 0), dxp)
        spread(1, s, [core])
        s = slot(hh, xp, k)
        have(1, s)
        send(X.at[1, s, 1], X.at[1, s, 1], half_sem(hh, 1), dxm)
        spread(1, s, [core])

    def far(hh):
        s = slot(hh, xa, k)
        got(X.at[1, s, 0], half_sem(hh, 0))
        got(X.at[1, s, 1], half_sem(hh, 1))
        spread(1, s, [core])

    def line_in(hh, i):
        for v in xs:
            s = slot(hh, v, k)
            have(0, s, (i,))
            spread(0, s, [core], (i,))

    def y_args(a, j):
        return (
            RA.at[a, j], RB.at[a, j],
            lambda i: rsA.at[a * 8 + j * 2 + i], lambda i: rsB.at[a * 16 + j * 4 + i], HALF,
        )

    order = list(zip(zs + [z], dz + [None]))

    def core_done(a):
        for hh in (h, nh):
            for v in (x, xm, xp, xa):
                have(a, slot(hh, v, nk))

    def start(a, i):
        j = order[i][0]
        lhs = ST[pl.ds(2 * j, 2)].reshape(256, 1024)
        PT[a, j] = dot(lhs, X[a].reshape(1024, CW)).astype(BF).reshape(4, ROWS, CW)
        ring_start(lambda v: PT.at[a, j, v], yp, ym, ya, dyp, dym, *y_args(a, j))

    def relay(a, i):
        j = order[i][0]
        ring_relay(lambda v: PT.at[a, j, v], yp, ym, dyp, dym, *y_args(a, j))

    def reduce_y(a, i):
        j, t = order[i]
        _, rb, _, sb, n = y_args(a, j)
        total = PT[a, j, y].astype(F32) + ring_sum(rb, sb, n)
        if t is None:
            KEEP[a] = total
        else:
            Q[a, j] = total.astype(BF)
            send(Q.at[a, j], RZ.at[a, z], rsRZ.at[a * 4 + z], t)

    def reduce_z(a):
        total = KEEP[a]
        for v in zs:
            got(RZ.at[a, v], rsRZ.at[a * 4 + v])
            total += RZ[a, v].astype(F32)
        return total

    across(0)
    spread(1, c, [dxp, dxm])
    line_in(h, 0)
    line_in(h, 1)
    across(1, (0,))
    line_in(nh, 0)
    line_in(nh, 1)
    core_done(0)
    start(0, 0)
    start(0, 1)
    start(0, 2)
    near(h)
    near(nh)
    relay(0, 0)
    start(0, 3)
    far(h)
    far(nh)
    relay(0, 1)
    core_done(1)
    start(1, 0)
    relay(0, 2)
    reduce_y(0, 0)
    start(1, 1)
    relay(0, 3)
    reduce_y(0, 1)
    start(1, 2)
    relay(1, 0)
    reduce_y(0, 2)
    start(1, 3)
    relay(1, 1)
    reduce_y(0, 3)
    relay(1, 2)
    reduce_y(1, 0)
    relay(1, 3)
    agg = reduce_z(0)
    loads[5].wait()
    loads[6].wait()
    agg_hi = agg.astype(BF)
    agg_lo = (agg - agg_hi.astype(F32)).astype(BF)
    both = dot(jnp.concatenate([agg_hi, agg_lo], axis=0), W1[...])
    v1 = both[:ROWS] + both[ROWS:]
    th = jnp.tanh(GELU_A * (v1 + GELU_B * v1 * v1 * v1))
    act = (0.5 * v1 * (1.0 + th)).astype(BF)
    dact = 0.5 * (1.0 + th) + 0.5 * v1 * (1.0 - th * th) * GELU_A * (1.0 + 3.0 * GELU_B * v1 * v1)
    Y[r] = dot(act, W2[...]).astype(BF)
    ACT[0] = dact
    GB[0, 0] = jnp.where(k == 0, agg_hi, act)
    GB[0, 1] = jnp.where(k == 0, agg_lo, jnp.zeros_like(agg_lo))
    GS[0] = jnp.where(k == 0, act, agg_hi)
    GS[1] = jnp.where(k == 0, jnp.zeros_like(agg_lo), agg_lo)

    reduce_y(1, 1)
    reduce_y(1, 2)
    reduce_y(1, 3)
    for t in dz + dy:
        send(Y.at[r], Y.at[r], rsY.at[r], t)
    bs = reduce_z(1).astype(BF)
    back = lax.dot_general(bs, W2[...], (((1,), (1,)), ((), ())), preferred_element_type=F32)
    bf = (back * ACT[0]).astype(BF)
    GB[0, 2] = jnp.where(k == 0, bf, bs)
    GS[2] = jnp.where(k == 0, bs, bf)
    send(GS, GB.at[1], rsGB.at[0], core)
    def pass_on(i):
        s = zs[i] * 4 + y
        got(Y.at[s], rsY.at[s])
        for t in dy:
            send(Y.at[s], Y.at[s], rsY.at[s], t)

    got(GB.at[1], rsGB.at[0])

    lhs = jnp.concatenate([GB[0, 0], GB[0, 1], GB[1, 0], GB[1, 1]], axis=0)
    rhs = jnp.concatenate([GB[0, 2], GB[0, 2], GB[1, 2], GB[1, 2]], axis=0)
    terms = lax.dot_general(lhs, rhs, (((0,), (0,)), ((), ())), preferred_element_type=F32)
    GT[...] = terms.astype(BF).reshape(4, 128, WIDTH)
    for v, t in zip(xs, dx):
        send(GT.at[v], GR.at[x], rsGR.at[x], t)

    for i in range(3):
        pass_on(i)
    total = GT[x].astype(F32)
    for v in xs:
        got(GR.at[v], rsGR.at[v])
        total += GR[v].astype(F32)
    GY[...] = total.reshape(4, 32, WIDTH)
    for v, t in zip(ys, dy):
        send(GY.at[v], RGY.at[y], rsRGY.at[y], t)
    total = GY[y]
    for v in ys:
        got(RGY.at[v], rsRGY.at[v])
        total += RGY[v]
    for u in range(4):
        for w in range(2):
            GZ[2 * u + w] = total[8 * u : 8 * u + 8, 256 * w : 256 * w + 256]
    for v, t in zip(qs, dq):
        send(GZ.at[v], RGZ.at[q], rsRGZ.at[q], t)

    for zz in zs + [z]:
        for v in ys:
            s = zz * 4 + v
            got(Y.at[s], rsY.at[s])
    def forward(hh):
        for i in range(2):
            prod = dot(S[pl.ds(hh * 4 + 2 * i, 2)].reshape(256, 1024), Y[...].reshape(1024, WIDTH))
            PO[pl.ds(hh * 8 + 4 * i, 4)] = prod.astype(BF).reshape(4, ROWS, WIDTH)
            for g in range(2):
                b = hh * 4 + 2 * i + g
                send(PO.at[2 * b + nk], RK.at[b], rsRK.at[b], core)

    def chip_sum(hh):
        for v, t in zip(xs + [x], dx + [None]):
            b = hh * 4 + v
            got(RK.at[b], rsRK.at[b])
            Q2[b] = (PO[2 * b + k].astype(F32) + RK[b].astype(F32)).astype(BF)
            if t is not None:
                send(Q2.at[b], OX.at[hh, x], rsOX.at[hh * 4 + x], t)

    def x_sum(hh):
        total = Q2[hh * 4 + x].astype(F32)
        for v in xs:
            got(OX.at[hh, v], rsOX.at[hh * 4 + v])
            total += OX[hh, v].astype(F32)
        return total

    forward(nh)
    forward(h)
    chip_sum(nh)
    chip_sum(h)

    total = GZ[q]
    for v in qs:
        got(RGZ.at[v], rsRGZ.at[v])
        total += RGZ[v]
    FZ[q] = total
    for t in dq:
        send(FZ.at[q], FZ.at[q], rsFZ.at[q], t)

    Q3[...] = x_sum(nh).astype(BF)
    send(Q3, RH, rsRH.at[0], anti)
    final = x_sum(h)
    for v in qs:
        got(FZ.at[v], rsFZ.at[v])
    for i in range(2):
        rows = []
        for u in range(2):
            rows.append(jnp.concatenate([FZ[4 * i + 2 * u], FZ[4 * i + 2 * u + 1]], axis=1))
        FG[k, x, y, i] = jnp.concatenate(rows, axis=0).astype(BF)
        for t in (dy, dx)[i]:
            send(FG.at[k, x, y, i], FG.at[k, x, y, i], rsFY.at[i * 4 + (y, x)[i]], t)

    def line(kk, i, v):
        return FG.at[kk, v, :, 0] if i == 0 else FG.at[kk, :, v, 1]

    got(RH, rsRH.at[0])
    OUT[...] = (final + RH[...].astype(F32)).astype(BF)
    store_out = pltpu.make_async_copy(OUT, out_hbm, lsem.at[7])
    store_out.start()
    for i in range(2):
        me = (x, y)[i]
        for v in (ys, xs)[i]:
            got(FG.at[k, x, v, 0] if i == 0 else FG.at[k, v, y, 1], rsFY.at[i * 4 + v])
        for t in (dx, dy)[i]:
            send(line(k, i, me), line(k, i, me), rsFX.at[i * 4 + me], t)
        send(line(k, i, me), line(k, i, me), rsFK.at[i * 4 + me], core)
    for d in range(3):
        for i in range(2):
            v = (xs, ys)[i][d]
            got(line(k, i, v), rsFX.at[i * 4 + v])
            send(line(k, i, v), line(k, i, v), rsFK.at[i * 4 + v], core)
    store_own = pltpu.make_async_copy(FG.at[k], grad_hbm.at[k], lsem.at[8])
    store_own.start()
    for i in range(2):
        for v in range(4):
            got(line(nk, i, v), rsFK.at[i * 4 + v])
    store_other = pltpu.make_async_copy(FG.at[nk], grad_hbm.at[nk], lsem.at[9])
    store_other.start()
    for cp in sends:
        cp.wait_send()
    store_out.wait()
    store_own.wait()
    store_other.wait()


def local(features, w_first, w_second, block_index, block_count, block_values, cotangent):
    index = block_index[0, 0][:LIVE]
    count = block_count[0, 0]
    ids = jnp.arange(LIVE, dtype=jnp.int32)
    places = jnp.arange(64, dtype=jnp.int32)
    hit = (index[None, :] == places[:, None]) & (ids < count)[None, :]
    table = LIVE + jnp.sum(jnp.where(hit, ids[None, :] - LIVE, 0), axis=1, dtype=jnp.int32)
    anyspace = pl.BlockSpec(memory_space=pl.ANY)
    vm = pltpu.VMEM
    dma = pltpu.SemaphoreType.DMA
    piece = (ROWS, WIDTH)
    chunk = (ROWS, CW)
    out, grads = pl.pallas_call(
        kernel,
        name="gcn",
        out_shape=(
            jax.ShapeDtypeStruct(piece, BF),
            jax.ShapeDtypeStruct((2, 4, 4, 2, 16, WIDTH), BF),
        ),
        in_specs=[pl.BlockSpec(memory_space=pltpu.SMEM)] + [anyspace] * 5,
        out_specs=(anyspace, anyspace),
        scratch_shapes=[
            vm((2, 16, 2, HALF, WIDTH), BF),
            vm((NCH, 4, 4) + chunk, BF),
            vm((NCH, 4, 2, HALF, CW), BF),
            vm((NCH, 4, 2) + chunk, BF),
            vm((NCH, 4) + chunk, BF),
            vm((NCH, 4) + chunk, BF),
            vm((NCH,) + chunk, F32),
            vm((16,) + piece, BF),
            vm((16,) + piece, BF),
            vm((8,) + piece, BF),
            vm((8,) + piece, BF),
            vm((2, 4) + piece, BF),
            vm(piece, BF),
            vm(piece, BF),
            vm((8, 128, 1024), BF),
            vm((8, 128, 1024), BF),
            vm((LIVE + 1, 128, 128), BF),
            vm((LIVE + 1, 128, 128), BF),
            vm((WIDTH, WIDTH), BF),
            vm((WIDTH, WIDTH), BF),
            vm((3,) + piece, BF),
            vm((2, 3) + piece, BF),
            vm((4, 128, WIDTH), BF),
            vm((4, 128, WIDTH), BF),
            vm((4, 32, WIDTH), F32),
            vm((4, 32, WIDTH), F32),
            vm((8, 8, 256), F32),
            vm((8, 8, 256), F32),
            vm((8, 8, 256), F32),
            vm((2, 4, 4, 2, 16, WIDTH), BF),
            vm((1,) + piece, F32),
            vm(piece, BF),
            dma((NSEND,)),
            dma((48,)),
            dma((4,)),
            dma((8 * NCH,)),
            dma((16 * NCH,)),
            dma((4 * NCH,)),
            dma((16,)),
            dma((8,)),
            dma((8,)),
            dma((1,)),
            dma((1,)),
            dma((4,)),
            dma((4,)),
            dma((8,)),
            dma((8,)),
            dma((8,)),
            dma((8,)),
            dma((8,)),
            dma((11,)),
        ],
        compiler_params=pltpu.CompilerParams(collective_id=0, has_side_effects=True),
    )(table, features, cotangent, w_first, w_second, block_values[0, 0])
    grads = grads.reshape(2, WIDTH, WIDTH).astype(F32)
    return out, grads[0], grads[1]


def solution(mesh):
    return jax.shard_map(
        local,
        mesh=mesh,
        in_specs=(
            P(("row", "col"), None),
            P(),
            P(),
            P("row", "col", None),
            P("row", "col"),
            P("row", "col", None, None, None),
            P(("row", "col"), None),
        ),
        out_specs=(P(("row", "col"), None), P(), P()),
        check_vma=False,
    )
```

time: 106 us -> 97.8 us (0.923)
  Pallas kernels: 96.3 us -> 91.4 us
  local copies, waits for them, and re-layouts: 8.23 us -> 4.12 us
    unnamed x11 -> x3, local copies, waits for them, and re-layouts: 5.97 us -> 0.63 us
    pallas_call x1, Pallas kernels: 96.3 us -> 91.4 us  [local(): pl.pallas_call(kernel, name='gcn', out_shape=(jax.ShapeDtypeStruct(piece,...]
    slice x1, local copies, waits for them, and re-layouts: 1.6 us -> 2.82 us  [local(): return (out, grads[0], grads[1])]
where the time goes in v2:
time: 97.8 us; the launch traced here: 97.5 us
  Pallas kernels  91.4 us (93%)
  local copies, waits for them, and re-layouts  4.12 us (4%)
  between operations  1.3 us (1%)
    pallas_call x1, Pallas kernels, local(): pl.pallas_call(kernel, name='gcn', out_shape=(jax.ShapeDtypeStruct(piece,...  91.4 us
    slice x1, local copies, waits for them, and re-layouts, local(): return (out, grads[0], grads[1])  2.82 us

profile of v2, /device:TPU:1, one launch (start us, length us, event | category | flops | bytes accessed | tf_op | source)
XLA Modules:
  0.0 97.5 jit_solution(4126949695335019861)
XLA Ops:
  1.3 0.7 slice_bitcast_fusion
  2.0 0.1 select_reduce_fusion
  2.0 0.5 broadcast_add_fusion.table
  2.6 91.4 %gcn.1 = (bf16[64,512]{1,0:T(8,128)(2,1)}, bf16[2,4,4,2,16,512]{5,4,3,2,1,0:T(8,128)(2,1)}) custom-call(s32[64]{0:T(128)} %broadcast_add_fusion.table, bf16[64,512]{1,0:T(8,128)(2,1)} %feat.1, bf16[64,512]{1,0:T(8,128)(2,1)} %cot.1, bf16[512,512]{1,0:T(8,128)(2,1)} %w1_hbm.1, bf16[512,512]{1,0:T(8,128)(2,1)} %w2_hbm.1, bf16[64,128,128]{2,1,0:T(8,128)(2,1)} %bitcast.7), custom_call_target="tpu_custom_call" | custom-call | tf_op jit(solution)/shard_map/gcn/pallas_call | solution.py:422
  94.0 0.0 copy-start
  94.0 2.8 %fusion.1 = (f32[1,4,4,2,16,512]{5,4,3,2,1,0:T(8,128)}, f32[1,4,4,2,16,512]{5,4,3,2,1,0:T(8,128)}) fusion(bf16[2,4,4,2,16,512]{5,4,3,2,1,0:T(8,128)(2,1)} %get-tuple-element.6), kind=kLoop, calls=%fused_computation.7 | loop fusion | bytes 4194304 | tf_op jit(solution)/shard_map/slice | solution.py:487
  96.8 0.0 copy-done
  96.8 0.6 copy.12
  (2 shorter events, 0.0 us)
Async XLA Ops:
  94.0 2.8 %copy-start = (bf16[64,512]{1,0:T(8,128)(2,1)S(1)}, bf16[64,512]{1,0:T(8,128)(2,1)}, u32[]{:S(2)}) copy-start(bf16[64,512]{1,0:T(8,128)(2,1)} %get-tuple-element.12) | copy-start | bytes 196612

commit v3 on v2

--- a/solution.py
+++ b/solution.py
@@ -20,16 +20,17 @@
 
 
 NCH = 2
-NSEND = 320
+NSEND = 360
 CW = 512
 HALF = ROWS // 2
+PART = WIDTH // 2
 
 
 def kernel(
-    table, feat, cot, w1_hbm, w2_hbm, vals_hbm, out_hbm, grad_hbm,
-    X, PT, RA, RB, Q, RZ, KEEP, Y, PO, RK, Q2, OX, Q3, RH, S, ST, V, VT, W1, W2,
-    GS, GB, GT, GR, GY, RGY, GZ, RGZ, FZ, FG, ACT, OUT,
-    ssem, rsX, rsXH, rsA, rsB, rsRZ, rsY, rsRK, rsOX, rsRH, rsGB, rsGR, rsRGY, rsRGZ,
+    index_hbm, count_hbm, feat, cot, w1_hbm, w2_hbm, vals_hbm, out_hbm, grad_hbm,
+    X, PT, RA, RB, RD, Q, RZ, KEEP, Y, PO, RK, Q2, OX, Q3, RH, S, ST, V, VT, W1, W2,
+    index, count, table, GS, GB, GT, GR, GF, GY, RGY, GZ, RGZ, FZ, FG, ACT, OUT,
+    ssem, rsX, rsXH, rsA, rsB, rsD, rsRZ, rsY, rsRK, rsOX, rsRH, rsGB, rsGR, rsRGY, rsRGZ,
     rsFZ, rsFY, rsFX, rsFK, lsem,
 ):
     r = lax.axis_index("row")
@@ -44,7 +45,8 @@
 
     xp, xm, xa = (x + 1) % 4, (x + 3) % 4, (x + 2) % 4
     yp, ym, ya = (y + 1) % 4, (y + 3) % 4, (y + 2) % 4
-    zs = [(z + d) % 4 for d in (1, 2, 3)]
+    zfar, znear = 3 * (1 - z // 2), 1 + z % 2
+    zs = [zfar, 6 - z - zfar - znear, znear]
     ys = [yp, ym, ya]
     qs = [(q + d) % 8 for d in (4, 3, 5, 2, 6, 1, 7)]
     core = dev(k=nk)
@@ -100,6 +102,8 @@
             loads.append(pltpu.make_async_copy(src, X.at[a, c, i], lsem.at[2 * a + i]))
     loads += [
         pltpu.make_async_copy(vals_hbm.at[pl.ds(0, LIVE)], V.at[pl.ds(0, LIVE)], lsem.at[10]),
+        pltpu.make_async_copy(index_hbm, index, lsem.at[6]),
+        pltpu.make_async_copy(count_hbm, count, lsem.at[7]),
         pltpu.make_async_copy(w1_hbm, W1, lsem.at[4]),
         pltpu.make_async_copy(w2_hbm, W2, lsem.at[5]),
     ]
@@ -136,6 +140,19 @@
     loads[3].wait()
     spread(1, c, [anti, core])
 
+    loads[5].wait()
+    loads[6].wait()
+    ids = [index[s] for s in range(LIVE)]
+    live = [s < count[0, 0] for s in range(LIVE)]
+
+    def find(p, carry):
+        at = jnp.int32(LIVE)
+        for s in range(LIVE):
+            at = jnp.where((ids[s] == p) & live[s], jnp.int32(s), at)
+        table[p] = at
+        return carry
+
+    lax.fori_loop(0, 64, find, 0)
     loads[4].wait()
     V[LIVE] = jnp.zeros((128, 128), BF)
     VT[LIVE] = jnp.zeros((128, 128), BF)
@@ -198,11 +215,15 @@
             for v in (x, xm, xp, xa):
                 have(a, slot(hh, v, nk))
 
+    def straight(a, i):
+        return a == 1 and i == 3
+
     def start(a, i):
         j = order[i][0]
         lhs = ST[pl.ds(2 * j, 2)].reshape(256, 1024)
         PT[a, j] = dot(lhs, X[a].reshape(1024, CW)).astype(BF).reshape(4, ROWS, CW)
-        ring_start(lambda v: PT.at[a, j, v], yp, ym, ya, dyp, dym, *y_args(a, j))
+        if not straight(a, i):
+            ring_start(lambda v: PT.at[a, j, v], yp, ym, ya, dyp, dym, *y_args(a, j))
 
     def relay(a, i):
         j = order[i][0]
@@ -211,7 +232,13 @@
     def reduce_y(a, i):
         j, t = order[i]
         _, rb, _, sb, n = y_args(a, j)
-        total = PT[a, j, y].astype(F32) + ring_sum(rb, sb, n)
+        total = PT[a, j, y].astype(F32)
+        if straight(a, i):
+            for v in ys:
+                got(RD.at[v], rsD.at[v])
+                total += RD[v].astype(F32)
+        else:
+            total += ring_sum(rb, sb, n)
         if t is None:
             KEEP[a] = total
         else:
@@ -257,11 +284,12 @@
     relay(1, 1)
     reduce_y(0, 3)
     relay(1, 2)
+    for v, t in zip(ys, dy):
+        send(PT.at[1, z, v], RD.at[y], rsD.at[y], t)
     reduce_y(1, 0)
-    relay(1, 3)
     agg = reduce_z(0)
-    loads[5].wait()
-    loads[6].wait()
+    loads[7].wait()
+    loads[8].wait()
     agg_hi = agg.astype(BF)
     agg_lo = (agg - agg_hi.astype(F32)).astype(BF)
     both = dot(jnp.concatenate([agg_hi, agg_lo], axis=0), W1[...])
@@ -269,7 +297,9 @@
     th = jnp.tanh(GELU_A * (v1 + GELU_B * v1 * v1 * v1))
     act = (0.5 * v1 * (1.0 + th)).astype(BF)
     dact = 0.5 * (1.0 + th) + 0.5 * v1 * (1.0 - th * th) * GELU_A * (1.0 + 3.0 * GELU_B * v1 * v1)
-    Y[r] = dot(act, W2[...]).astype(BF)
+    linear = dot(act, W2[...]).astype(BF)
+    for e in range(2):
+        Y[e, r] = linear[:, e * PART : (e + 1) * PART]
     ACT[0] = dact
     GB[0, 0] = jnp.where(k == 0, agg_hi, act)
     GB[0, 1] = jnp.where(k == 0, agg_lo, jnp.zeros_like(agg_lo))
@@ -279,186 +309,211 @@
     reduce_y(1, 1)
     reduce_y(1, 2)
     reduce_y(1, 3)
-    for t in dz + dy:
-        send(Y.at[r], Y.at[r], rsY.at[r], t)
     bs = reduce_z(1).astype(BF)
     back = lax.dot_general(bs, W2[...], (((1,), (1,)), ((), ())), preferred_element_type=F32)
     bf = (back * ACT[0]).astype(BF)
     GB[0, 2] = jnp.where(k == 0, bf, bs)
     GS[2] = jnp.where(k == 0, bs, bf)
     send(GS, GB.at[1], rsGB.at[0], core)
-    def pass_on(i):
-        s = zs[i] * 4 + y
-        got(Y.at[s], rsY.at[s])
-        for t in dy:
-            send(Y.at[s], Y.at[s], rsY.at[s], t)
+    for e in range(2):
+        for t in dz:
+            send(Y.at[e, r], Y.at[e, r], rsY.at[e * 16 + r], t)
+
+    def pass_on(e):
+        for v in zs:
+            s = v * 4 + y
+            got(Y.at[e, s], rsY.at[e * 16 + s])
+            for t in dy:
+                send(Y.at[e, s], Y.at[e, s], rsY.at[e * 16 + s], t)
 
     got(GB.at[1], rsGB.at[0])
 
     lhs = jnp.concatenate([GB[0, 0], GB[0, 1], GB[1, 0], GB[1, 1]], axis=0)
     rhs = jnp.concatenate([GB[0, 2], GB[0, 2], GB[1, 2], GB[1, 2]], axis=0)
     terms = lax.dot_general(lhs, rhs, (((0,), (0,)), ((), ())), preferred_element_type=F32)
-    GT[...] = terms.astype(BF).reshape(4, 128, WIDTH)
-    for v, t in zip(xs, dx):
-        send(GT.at[v], GR.at[x], rsGR.at[x], t)
-
-    for i in range(3):
-        pass_on(i)
-    total = GT[x].astype(F32)
-    for v in xs:
-        got(GR.at[v], rsGR.at[v])
-        total += GR[v].astype(F32)
-    GY[...] = total.reshape(4, 32, WIDTH)
-    for v, t in zip(ys, dy):
-        send(GY.at[v], RGY.at[y], rsRGY.at[y], t)
-    total = GY[y]
-    for v in ys:
-        got(RGY.at[v], rsRGY.at[v])
-        total += RGY[v]
-    for u in range(4):
-        for w in range(2):
-            GZ[2 * u + w] = total[8 * u : 8 * u + 8, 256 * w : 256 * w + 256]
+    GT[...] = terms.astype(BF).reshape(2, 4, ROWS, WIDTH)
+    sides = ((x, xs, dx), (y, ys, dy))
+    for i in range(2):
+        me, others, devs = sides[i]
+        for v, t in zip(others, devs):
+            send(GT.at[i, v], GR.at[i, me], rsGR.at[i * 4 + me], t)
+
+    for e in range(2):
+        for t in dy:
+            send(Y.at[e, r], Y.at[e, r], rsY.at[e * 16 + r], t)
+    for i in range(2):
+        me, others, _ = sides[i]
+        total = GT[i, me].astype(F32)
+        for v in others:
+            got(GR.at[i, v], rsGR.at[i * 4 + v])
+            total += GR[i, v].astype(F32)
+        GF[i] = total.reshape(4, 16, WIDTH)
+        GY[i] = total.astype(BF).reshape(4, 16, WIDTH)
+        me, others, devs = sides[1 - i]
+        for v, t in zip(others, devs):
+            send(GY.at[i, v], RGY.at[i, me], rsRGY.at[i * 4 + me], t)
+    pass_on(0)
+    pass_on(1)
+    for i in range(2):
+        me, others, _ = sides[1 - i]
+        total = GF[i, me]
+        for v in others:
+            got(RGY.at[i, v], rsRGY.at[i * 4 + v])
+            total += RGY[i, v].astype(F32)
+        for w in range(4):
+            GZ[4 * i + w] = total[:, 128 * w : 128 * w + 128]
     for v, t in zip(qs, dq):
         send(GZ.at[v], RGZ.at[q], rsRGZ.at[q], t)
 
-    for zz in zs + [z]:
-        for v in ys:
-            s = zz * 4 + v
-            got(Y.at[s], rsY.at[s])
-    def forward(hh):
+    def forward(e):
+        for zz in zs + [z]:
+            for v in ys:
+                s = zz * 4 + v
+                got(Y.at[e, s], rsY.at[e * 16 + s])
         for i in range(2):
-            prod = dot(S[pl.ds(hh * 4 + 2 * i, 2)].reshape(256, 1024), Y[...].reshape(1024, WIDTH))
-            PO[pl.ds(hh * 8 + 4 * i, 4)] = prod.astype(BF).reshape(4, ROWS, WIDTH)
-            for g in range(2):
-                b = hh * 4 + 2 * i + g
-                send(PO.at[2 * b + nk], RK.at[b], rsRK.at[b], core)
-
-    def chip_sum(hh):
-        for v, t in zip(xs + [x], dx + [None]):
-            b = hh * 4 + v
-            got(RK.at[b], rsRK.at[b])
-            Q2[b] = (PO[2 * b + k].astype(F32) + RK[b].astype(F32)).astype(BF)
-            if t is not None:
-                send(Q2.at[b], OX.at[hh, x], rsOX.at[hh * 4 + x], t)
-
-    def x_sum(hh):
-        total = Q2[hh * 4 + x].astype(F32)
-        for v in xs:
-            got(OX.at[hh, v], rsOX.at[hh * 4 + v])
-            total += OX[hh, v].astype(F32)
+            prod = dot(S[pl.ds(4 * i, 4)].reshape(512, 1024), Y[e].reshape(1024, PART))
+            PO[e, pl.ds(8 * i, 8)] = prod.astype(BF).reshape(8, ROWS, PART)
+            for g in range(4):
+                b = 4 * i + g
+                send(PO.at[e, 2 * b + nk], RK.at[e, b], rsRK.at[e * 8 + b], core)
+
+    def chip_sum(e):
+        for hh in (nh, h):
+            for v, t in zip(xs + [x], dx + [None]):
+                b = hh * 4 + v
+                got(RK.at[e, b], rsRK.at[e * 8 + b])
+                Q2[e, b] = (PO[e, 2 * b + k].astype(F32) + RK[e, b].astype(F32)).astype(BF)
+                if t is not None:
+                    send(Q2.at[e, b], OX.at[e, hh, x], rsOX.at[e * 8 + hh * 4 + x], t)
+
+    def x_sum(e):
+        sums = []
+        for hh in (nh, h):
+            total = Q2[e, hh * 4 + x].astype(F32)
+            for v in xs:
+                got(OX.at[e, hh, v], rsOX.at[e * 8 + hh * 4 + v])
+                total += OX[e, hh, v].astype(F32)
+            if hh is nh:
+                Q3[e] = total.astype(BF)
+                send(Q3.at[e], RH.at[e], rsRH.at[e], anti)
         return total
 
-    forward(nh)
-    forward(h)
-    chip_sum(nh)
-    chip_sum(h)
-
+    def finish(e, total):
+        got(RH.at[e], rsRH.at[e])
+        OUT[:, e * PART : (e + 1) * PART] = (total + RH[e].astype(F32)).astype(BF)
+
+    forward(0)
     total = GZ[q]
     for v in qs:
         got(RGZ.at[v], rsRGZ.at[v])
         total += RGZ[v]
-    FZ[q] = total
+    FZ[q] = total.astype(BF)
     for t in dq:
         send(FZ.at[q], FZ.at[q], rsFZ.at[q], t)
-
-    Q3[...] = x_sum(nh).astype(BF)
-    send(Q3, RH, rsRH.at[0], anti)
-    final = x_sum(h)
+    chip_sum(0)
+    forward(1)
+
     for v in qs:
         got(FZ.at[v], rsFZ.at[v])
     for i in range(2):
-        rows = []
-        for u in range(2):
-            rows.append(jnp.concatenate([FZ[4 * i + 2 * u], FZ[4 * i + 2 * u + 1]], axis=1))
-        FG[k, x, y, i] = jnp.concatenate(rows, axis=0).astype(BF)
-        for t in (dy, dx)[i]:
-            send(FG.at[k, x, y, i], FG.at[k, x, y, i], rsFY.at[i * 4 + (y, x)[i]], t)
-
-    def line(kk, i, v):
-        return FG.at[kk, v, :, 0] if i == 0 else FG.at[kk, :, v, 1]
-
-    got(RH, rsRH.at[0])
-    OUT[...] = (final + RH[...].astype(F32)).astype(BF)
-    store_out = pltpu.make_async_copy(OUT, out_hbm, lsem.at[7])
-    store_out.start()
-    for i in range(2):
-        me = (x, y)[i]
-        for v in (ys, xs)[i]:
-            got(FG.at[k, x, v, 0] if i == 0 else FG.at[k, v, y, 1], rsFY.at[i * 4 + v])
-        for t in (dx, dy)[i]:
-            send(line(k, i, me), line(k, i, me), rsFX.at[i * 4 + me], t)
-        send(line(k, i, me), line(k, i, me), rsFK.at[i * 4 + me], core)
+        outer, inner = (x, y) if i == 0 else (y, x)
+        FG[k, i, outer, inner] = jnp.concatenate([FZ[4 * i + w] for w in range(4)], axis=1)
+        for t in sides[1 - i][2]:
+            send(FG.at[k, i, outer, inner], FG.at[k, i, outer, inner], rsFY.at[i * 4 + inner], t)
+
+    chip_sum(1)
+    first_half = x_sum(0)
+    for i in range(2):
+        me, _, devs = sides[i]
+        for v in sides[1 - i][1]:
+            got(FG.at[k, i, me, v], rsFY.at[i * 4 + v])
+        for t in devs:
+            send(FG.at[k, i, me], FG.at[k, i, me], rsFX.at[i * 4 + me], t)
+        send(FG.at[k, i, me], FG.at[k, i, me], rsFK.at[i * 4 + me], core)
+
+    stores = []
+
+    def store(kk, i, v):
+        cp = pltpu.make_async_copy(FG.at[kk, i, v], grad_hbm.at[kk, i, v], lsem.at[len(stores)])
+        cp.start()
+        stores.append(cp)
+
+    second_half = x_sum(1)
+    finish(0, first_half)
     for d in range(3):
         for i in range(2):
-            v = (xs, ys)[i][d]
-            got(line(k, i, v), rsFX.at[i * 4 + v])
-            send(line(k, i, v), line(k, i, v), rsFK.at[i * 4 + v], core)
-    store_own = pltpu.make_async_copy(FG.at[k], grad_hbm.at[k], lsem.at[8])
-    store_own.start()
+            v = sides[i][1][d]
+            got(FG.at[k, i, v], rsFX.at[i * 4 + v])
+            send(FG.at[k, i, v], FG.at[k, i, v], rsFK.at[i * 4 + v], core)
     for i in range(2):
         for v in range(4):
-            got(line(nk, i, v), rsFK.at[i * 4 + v])
-    store_other = pltpu.make_async_copy(FG.at[nk], grad_hbm.at[nk], lsem.at[9])
-    store_other.start()
+            store(k, i, v)
+    for i in range(2):
+        for v in (sides[i][0], *sides[i][1]):
+            got(FG.at[nk, i, v], rsFK.at[i * 4 + v])
+            store(nk, i, v)
+    finish(1, second_half)
+    store_out = pltpu.make_async_copy(OUT, out_hbm, lsem.at[16])
+    store_out.start()
     for cp in sends:
         cp.wait_send()
     store_out.wait()
-    store_own.wait()
-    store_other.wait()
+    for cp in stores:
+        cp.wait()
 
 
 def local(features, w_first, w_second, block_index, block_count, block_values, cotangent):
-    index = block_index[0, 0][:LIVE]
-    count = block_count[0, 0]
-    ids = jnp.arange(LIVE, dtype=jnp.int32)
-    places = jnp.arange(64, dtype=jnp.int32)
-    hit = (index[None, :] == places[:, None]) & (ids < count)[None, :]
-    table = LIVE + jnp.sum(jnp.where(hit, ids[None, :] - LIVE, 0), axis=1, dtype=jnp.int32)
     anyspace = pl.BlockSpec(memory_space=pl.ANY)
     vm = pltpu.VMEM
     dma = pltpu.SemaphoreType.DMA
     piece = (ROWS, WIDTH)
     chunk = (ROWS, CW)
+    part = (ROWS, PART)
     out, grads = pl.pallas_call(
         kernel,
         name="gcn",
         out_shape=(
             jax.ShapeDtypeStruct(piece, BF),
-            jax.ShapeDtypeStruct((2, 4, 4, 2, 16, WIDTH), BF),
+            jax.ShapeDtypeStruct((2, 2, 4, 4, 16, WIDTH), BF),
         ),
-        in_specs=[pl.BlockSpec(memory_space=pltpu.SMEM)] + [anyspace] * 5,
+        in_specs=[anyspace] * 7,
         out_specs=(anyspace, anyspace),
         scratch_shapes=[
             vm((2, 16, 2, HALF, WIDTH), BF),
             vm((NCH, 4, 4) + chunk, BF),
             vm((NCH, 4, 2, HALF, CW), BF),
             vm((NCH, 4, 2) + chunk, BF),
+            vm((4,) + piece, BF),
             vm((NCH, 4) + chunk, BF),
             vm((NCH, 4) + chunk, BF),
             vm((NCH,) + chunk, F32),
-            vm((16,) + piece, BF),
-            vm((16,) + piece, BF),
-            vm((8,) + piece, BF),
-            vm((8,) + piece, BF),
-            vm((2, 4) + piece, BF),
-            vm(piece, BF),
-            vm(piece, BF),
+            vm((2, 16) + part, BF),
+            vm((2, 16) + part, BF),
+            vm((2, 8) + part, BF),
+            vm((2, 8) + part, BF),
+            vm((2, 2, 4) + part, BF),
+            vm((2,) + part, BF),
+            vm((2,) + part, BF),
             vm((8, 128, 1024), BF),
             vm((8, 128, 1024), BF),
             vm((LIVE + 1, 128, 128), BF),
             vm((LIVE + 1, 128, 128), BF),
             vm((WIDTH, WIDTH), BF),
             vm((WIDTH, WIDTH), BF),
+            pltpu.SMEM((64,), jnp.int32),
+            pltpu.SMEM((1, 1), jnp.int32),
+            pltpu.SMEM((64,), jnp.int32),
             vm((3,) + piece, BF),
             vm((2, 3) + piece, BF),
-            vm((4, 128, WIDTH), BF),
-            vm((4, 128, WIDTH), BF),
-            vm((4, 32, WIDTH), F32),
-            vm((4, 32, WIDTH), F32),
-            vm((8, 8, 256), F32),
-            vm((8, 8, 256), F32),
-            vm((8, 8, 256), F32),
-            vm((2, 4, 4, 2, 16, WIDTH), BF),
+            vm((2, 4) + piece, BF),
+            vm((2, 4) + piece, BF),
+            vm((2, 4, 16, WIDTH), F32),
+            vm((2, 4, 16, WIDTH), BF),
+            vm((2, 4, 16, WIDTH), BF),
+            vm((8, 16, 128), F32),
+            vm((8, 16, 128), F32),
+            vm((8, 16, 128), BF),
+            vm((2, 2, 4, 4, 16, WIDTH), BF),
             vm((1,) + piece, F32),
             vm(piece, BF),
             dma((NSEND,)),
@@ -466,23 +521,24 @@
             dma((4,)),
             dma((8 * NCH,)),
             dma((16 * NCH,)),
+            dma((4,)),
             dma((4 * NCH,)),
+            dma((32,)),
             dma((16,)),
-            dma((8,)),
-            dma((8,)),
+            dma((16,)),
+            dma((2,)),
             dma((1,)),
-            dma((1,)),
-            dma((4,)),
-            dma((4,)),
-            dma((8,)),
-            dma((8,)),
-            dma((8,)),
-            dma((8,)),
-            dma((8,)),
-            dma((11,)),
+            dma((8,)),
+            dma((8,)),
+            dma((8,)),
+            dma((8,)),
+            dma((8,)),
+            dma((8,)),
+            dma((8,)),
+            dma((17,)),
         ],
         compiler_params=pltpu.CompilerParams(collective_id=0, has_side_effects=True),
-    )(table, features, cotangent, w_first, w_second, block_values[0, 0])
+    )(block_index[0, 0], block_count, features, cotangent, w_first, w_second, block_values[0, 0])
     grads = grads.reshape(2, WIDTH, WIDTH).astype(F32)
     return out, grads[0], grads[1]
 

time: 97.8 us -> 89.5 us (0.915)
  Pallas kernels: 91.4 us -> 84.6 us
    pallas_call x1, Pallas kernels: 91.4 us -> 84.6 us  [local(): pl.pallas_call(kernel, name='gcn', out_shape=(jax.ShapeDtypeStruct(piece,...]
where the time goes in v3:
time: 89.5 us; the launch traced here: 89.3 us
  Pallas kernels  84.6 us (95%)
  local copies, waits for them, and re-layouts  3.47 us (4%)
  between operations  1.3 us (1%)
    pallas_call x1, Pallas kernels, local(): pl.pallas_call(kernel, name='gcn', out_shape=(jax.ShapeDtypeStruct(piece,...  84.6 us
    slice x1, local copies, waits for them, and re-layouts, local(): return (out, grads[0], grads[1])  2.84 us

profile of v3, /device:TPU:1, one launch (start us, length us, event | category | flops | bytes accessed | tf_op | source)
XLA Modules:
  0.0 89.3 jit_solution(12536857027969501696)
XLA Ops:
  1.3 84.6 %gcn.1 = (bf16[64,512]{1,0:T(8,128)(2,1)}, bf16[2,2,4,4,16,512]{5,4,3,2,1,0:T(8,128)(2,1)}) custom-call(s32[64]{0:T(128)} %bitcast.7, s32[1,1]{1,0:T(1,128)S(6)} %copy.11.count_hbm, bf16[64,512]{1,0:T(8,128)(2,1)} %feat.1, bf16[64,512]{1,0:T(8,128)(2,1)} %cot.1, bf16[512,512]{1,0:T(8,128)(2,1)} %w1_hbm.1, bf16[512,512]{1,0:T(8,128)(2,1)} %w2_hbm.1, ...), custom_call_target="tpu_custom_call" | custom-call | tf_op jit(solution)/shard_map/gcn/pallas_call | solution.py:472
  85.9 0.0 copy-start
  85.9 2.8 %fusion = (f32[1,2,4,4,16,512]{5,4,3,2,1,0:T(8,128)}, f32[1,2,4,4,16,512]{5,4,3,2,1,0:T(8,128)}) fusion(bf16[2,2,4,4,16,512]{5,4,3,2,1,0:T(8,128)(2,1)} %get-tuple-element.6), kind=kLoop, calls=%fused_computation | loop fusion | bytes 4194304 | tf_op jit(solution)/shard_map/slice | solution.py:543
  88.7 0.0 copy-done
  88.7 0.6 copy.12
Async XLA Ops:
  85.9 2.8 %copy-start = (bf16[64,512]{1,0:T(8,128)(2,1)S(1)}, bf16[64,512]{1,0:T(8,128)(2,1)}, u32[]{:S(2)}) copy-start(bf16[64,512]{1,0:T(8,128)(2,1)} %get-tuple-element.12) | copy-start | bytes 196612

commit v4 on v3

--- a/solution.py
+++ b/solution.py
@@ -277,16 +277,18 @@
     start(1, 1)
     relay(0, 3)
     reduce_y(0, 1)
+    relay(1, 0)
     start(1, 2)
-    relay(1, 0)
     reduce_y(0, 2)
     start(1, 3)
     relay(1, 1)
-    reduce_y(0, 3)
     relay(1, 2)
     for v, t in zip(ys, dy):
         send(PT.at[1, z, v], RD.at[y], rsD.at[y], t)
     reduce_y(1, 0)
+    reduce_y(1, 1)
+    reduce_y(1, 2)
+    reduce_y(0, 3)
     agg = reduce_z(0)
     loads[7].wait()
     loads[8].wait()
@@ -305,16 +307,15 @@
     GB[0, 1] = jnp.where(k == 0, agg_lo, jnp.zeros_like(agg_lo))
     GS[0] = jnp.where(k == 0, act, agg_hi)
     GS[1] = jnp.where(k == 0, jnp.zeros_like(agg_lo), agg_lo)
-
-    reduce_y(1, 1)
-    reduce_y(1, 2)
+    send(GS.at[:2], GB.at[1, :2], rsGB.at[1], core)
+
     reduce_y(1, 3)
     bs = reduce_z(1).astype(BF)
     back = lax.dot_general(bs, W2[...], (((1,), (1,)), ((), ())), preferred_element_type=F32)
     bf = (back * ACT[0]).astype(BF)
     GB[0, 2] = jnp.where(k == 0, bf, bs)
     GS[2] = jnp.where(k == 0, bs, bf)
-    send(GS, GB.at[1], rsGB.at[0], core)
+    send(GS.at[2], GB.at[1, 2], rsGB.at[0], core)
     for e in range(2):
         for t in dz:
             send(Y.at[e, r], Y.at[e, r], rsY.at[e * 16 + r], t)
@@ -326,7 +327,8 @@
             for t in dy:
                 send(Y.at[e, s], Y.at[e, s], rsY.at[e * 16 + s], t)
 
-    got(GB.at[1], rsGB.at[0])
+    got(GB.at[1, :2], rsGB.at[1])
+    got(GB.at[1, 2], rsGB.at[0])
 
     lhs = jnp.concatenate([GB[0, 0], GB[0, 1], GB[1, 0], GB[1, 1]], axis=0)
     rhs = jnp.concatenate([GB[0, 2], GB[0, 2], GB[1, 2], GB[1, 2]], axis=0)
@@ -402,7 +404,6 @@
         got(RH.at[e], rsRH.at[e])
         OUT[:, e * PART : (e + 1) * PART] = (total + RH[e].astype(F32)).astype(BF)
 
-    forward(0)
     total = GZ[q]
     for v in qs:
         got(RGZ.at[v], rsRGZ.at[v])
@@ -410,8 +411,8 @@
     FZ[q] = total.astype(BF)
     for t in dq:
         send(FZ.at[q], FZ.at[q], rsFZ.at[q], t)
+    forward(0)
     chip_sum(0)
-    forward(1)
 
     for v in qs:
         got(FZ.at[v], rsFZ.at[v])
@@ -421,8 +422,8 @@
         for t in sides[1 - i][2]:
             send(FG.at[k, i, outer, inner], FG.at[k, i, outer, inner], rsFY.at[i * 4 + inner], t)
 
+    forward(1)
     chip_sum(1)
-    first_half = x_sum(0)
     for i in range(2):
         me, _, devs = sides[i]
         for v in sides[1 - i][1]:
@@ -438,6 +439,7 @@
         cp.start()
         stores.append(cp)
 
+    first_half = x_sum(0)
     second_half = x_sum(1)
     finish(0, first_half)
     for d in range(3):
@@ -527,7 +529,7 @@
             dma((16,)),
             dma((16,)),
             dma((2,)),
-            dma((1,)),
+            dma((2,)),
             dma((8,)),
             dma((8,)),
             dma((8,)),

time: 89.5 us -> 88.4 us (0.988)
  Pallas kernels: 84.6 us -> 83.6 us
    pallas_call x1, Pallas kernels: 84.6 us -> 83.6 us  [local(): pl.pallas_call(kernel, name='gcn', out_shape=(jax.ShapeDtypeStruct(piece,...]
where the time goes in v4:
time: 88.4 us; the launch traced here: 88.3 us
  Pallas kernels  83.6 us (95%)
  local copies, waits for them, and re-layouts  3.47 us (4%)
  between operations  1.3 us (1%)
    pallas_call x1, Pallas kernels, local(): pl.pallas_call(kernel, name='gcn', out_shape=(jax.ShapeDtypeStruct(piece,...  83.6 us
    slice x1, local copies, waits for them, and re-layouts, local(): return (out, grads[0], grads[1])  2.84 us

profile of v4, /device:TPU:1, one launch (start us, length us, event | category | flops | bytes accessed | tf_op | source)
XLA Modules:
  0.0 88.3 jit_solution(14784580857643339824)
XLA Ops:
  1.3 83.6 %gcn.1 = (bf16[64,512]{1,0:T(8,128)(2,1)}, bf16[2,2,4,4,16,512]{5,4,3,2,1,0:T(8,128)(2,1)}) custom-call(s32[64]{0:T(128)} %bitcast.7, s32[1,1]{1,0:T(1,128)S(6)} %copy.11.count_hbm, bf16[64,512]{1,0:T(8,128)(2,1)} %feat.1, bf16[64,512]{1,0:T(8,128)(2,1)} %cot.1, bf16[512,512]{1,0:T(8,128)(2,1)} %w1_hbm.1, bf16[512,512]{1,0:T(8,128)(2,1)} %w2_hbm.1, ...), custom_call_target="tpu_custom_call" | custom-call | tf_op jit(solution)/shard_map/gcn/pallas_call | solution.py:474
  84.9 0.0 copy-start
  84.9 2.8 %fusion = (f32[1,2,4,4,16,512]{5,4,3,2,1,0:T(8,128)}, f32[1,2,4,4,16,512]{5,4,3,2,1,0:T(8,128)}) fusion(bf16[2,2,4,4,16,512]{5,4,3,2,1,0:T(8,128)(2,1)} %get-tuple-element.6), kind=kLoop, calls=%fused_computation | loop fusion | bytes 4194304 | tf_op jit(solution)/shard_map/slice | solution.py:545
  87.7 0.0 copy-done
  87.7 0.6 copy.12
Async XLA Ops:
  84.9 2.8 %copy-start = (bf16[64,512]{1,0:T(8,128)(2,1)S(1)}, bf16[64,512]{1,0:T(8,128)(2,1)}, u32[]{:S(2)}) copy-start(bf16[64,512]{1,0:T(8,128)(2,1)} %get-tuple-element.12) | copy-start | bytes 196612

commit v5 on v4

--- a/solution.py
+++ b/solution.py
@@ -332,10 +332,12 @@
 
     lhs = jnp.concatenate([GB[0, 0], GB[0, 1], GB[1, 0], GB[1, 1]], axis=0)
     rhs = jnp.concatenate([GB[0, 2], GB[0, 2], GB[1, 2], GB[1, 2]], axis=0)
-    terms = lax.dot_general(lhs, rhs, (((0,), (0,)), ((), ())), preferred_element_type=F32)
-    GT[...] = terms.astype(BF).reshape(2, 4, ROWS, WIDTH)
     sides = ((x, xs, dx), (y, ys, dy))
     for i in range(2):
+        terms = lax.dot_general(
+            lhs[:, 256 * i : 256 * i + 256], rhs, (((0,), (0,)), ((), ())), preferred_element_type=F32
+        )
+        GT[i] = terms.astype(BF).reshape(4, ROWS, WIDTH)
         me, others, devs = sides[i]
         for v, t in zip(others, devs):
             send(GT.at[i, v], GR.at[i, me], rsGR.at[i * 4 + me], t)
@@ -363,7 +365,7 @@
             got(RGY.at[i, v], rsRGY.at[i * 4 + v])
             total += RGY[i, v].astype(F32)
         for w in range(4):
-            GZ[4 * i + w] = total[:, 128 * w : 128 * w + 128]
+            GZ[4 * i + w] = total[:, 128 * w : 128 * w + 128].astype(BF)
     for v, t in zip(qs, dq):
         send(GZ.at[v], RGZ.at[q], rsRGZ.at[q], t)
 
@@ -404,10 +406,10 @@
         got(RH.at[e], rsRH.at[e])
         OUT[:, e * PART : (e + 1) * PART] = (total + RH[e].astype(F32)).astype(BF)
 
-    total = GZ[q]
+    total = GZ[q].astype(F32)
     for v in qs:
         got(RGZ.at[v], rsRGZ.at[v])
-        total += RGZ[v]
+        total += RGZ[v].astype(F32)
     FZ[q] = total.astype(BF)
     for t in dq:
         send(FZ.at[q], FZ.at[q], rsFZ.at[q], t)
@@ -512,8 +514,8 @@
             vm((2, 4, 16, WIDTH), F32),
             vm((2, 4, 16, WIDTH), BF),
             vm((2, 4, 16, WIDTH), BF),
-            vm((8, 16, 128), F32),
-            vm((8, 16, 128), F32),
+            vm((8, 16, 128), BF),
+            vm((8, 16, 128), BF),
             vm((8, 16, 128), BF),
             vm((2, 2, 4, 4, 16, WIDTH), BF),
             vm((1,) + piece, F32),

time: 88.4 us -> 88.3 us (level)
  no operation moved by 1% of the time
where the time goes in v5:
time: 88.3 us; the launch traced here: 88.2 us
  Pallas kernels  83.5 us (95%)
  local copies, waits for them, and re-layouts  3.47 us (4%)
  between operations  1.3 us (1%)
    pallas_call x1, Pallas kernels, local(): pl.pallas_call(kernel, name='gcn', out_shape=(jax.ShapeDtypeStruct(piece,...  83.5 us
    slice x1, local copies, waits for them, and re-layouts, local(): return (out, grads[0], grads[1])  2.84 us

profile of v5, /device:TPU:1, one launch (start us, length us, event | category | flops | bytes accessed | tf_op | source)
XLA Modules:
  0.0 88.2 jit_solution(13749974514075630686)
XLA Ops:
  1.3 83.5 %gcn.1 = (bf16[64,512]{1,0:T(8,128)(2,1)}, bf16[2,2,4,4,16,512]{5,4,3,2,1,0:T(8,128)(2,1)}) custom-call(s32[64]{0:T(128)} %bitcast.7, s32[1,1]{1,0:T(1,128)S(6)} %copy.11.count_hbm, bf16[64,512]{1,0:T(8,128)(2,1)} %feat.1, bf16[64,512]{1,0:T(8,128)(2,1)} %cot.1, bf16[512,512]{1,0:T(8,128)(2,1)} %w1_hbm.1, bf16[512,512]{1,0:T(8,128)(2,1)} %w2_hbm.1, ...), custom_call_target="tpu_custom_call" | custom-call | tf_op jit(solution)/shard_map/gcn/pallas_call | solution.py:476
  84.8 0.0 copy-start
  84.8 2.8 %fusion = (f32[1,2,4,4,16,512]{5,4,3,2,1,0:T(8,128)}, f32[1,2,4,4,16,512]{5,4,3,2,1,0:T(8,128)}) fusion(bf16[2,2,4,4,16,512]{5,4,3,2,1,0:T(8,128)(2,1)} %get-tuple-element.6), kind=kLoop, calls=%fused_computation | loop fusion | bytes 4194304 | tf_op jit(solution)/shard_map/slice | solution.py:547
  87.6 0.0 copy-done
  87.6 0.6 copy.12
Async XLA Ops:
  84.8 2.8 %copy-start = (bf16[64,512]{1,0:T(8,128)(2,1)S(1)}, bf16[64,512]{1,0:T(8,128)(2,1)}, u32[]{:S(2)}) copy-start(bf16[64,512]{1,0:T(8,128)(2,1)} %get-tuple-element.12) | copy-start | bytes 196612
